TPU v7x, 32 devices: a whole 2x2x4 slice. The times are simulated.
32 devices in a mesh: rep: 8 (over y, x, core), shard: 4 (over z).
Axes of the slice: x: 2, y: 2, z: 4, core: 2. Of those that a mesh axis runs over, the one named last changes fastest.
Arguments:
- layer_input: bfloat16 [16384, 2048], P(('rep', 'shard')), may hold values from -6 to 6
- gain_attn: bfloat16 [2048], P('shard'), may hold values from 0.5 to 1.5
- w_query: bfloat16 [2048, 2048], P('shard'), may hold values from -0.125 to 0.125
- w_key: bfloat16 [2048, 2048], P('shard'), may hold values from -0.125 to 0.125
- w_value: bfloat16 [2048, 2048], P('shard'), may hold values from -0.125 to 0.125
- w_out: bfloat16 [2048, 2048], P(None, 'shard'), may hold values from -0.5 to 0.5
- gain_mlp: bfloat16 [2048], P('shard'), may hold values from 0.5 to 1.5
- w_gate: bfloat16 [2048, 5632], P('shard'), may hold values from -0.125 to 0.125
- w_up: bfloat16 [2048, 5632], P('shard'), may hold values from -0.125 to 0.125
- w_down: bfloat16 [5632, 2048], P(None, 'shard'), may hold values from -0.078125 to 0.078125
- segments: int32 [32, 512], P(('rep', 'shard')), may hold values from 0 to 3, never falling along the last dimension, each value on 1 to 256 neighbouring positions
- attn_route: int32 [16384, 2], P(('rep', 'shard')), may hold values from 0 to 7, all different within a row
- attn_gate: float32 [16384, 2], P(('rep', 'shard')), may hold values from 0.2 to 1
- mlp_route: int32 [16384, 2], P(('rep', 'shard')), may hold values from 0 to 7, all different within a row
- mlp_gate: float32 [16384, 2], P(('rep', 'shard')), may hold values from 0.2 to 1
- cotangent: bfloat16 [16384, 2048], P(('rep', 'shard')), may hold values from -6 to 6
Outputs:
- output: bfloat16 [16384, 2048], P(('rep', 'shard'))
- grad_input: bfloat16 [16384, 2048], P(('rep', 'shard'))
- grad_gain_attn: float32 [2048], P('shard')
- grad_query: float32 [2048, 2048], P('shard')
- grad_key: float32 [2048, 2048], P('shard')
- grad_value: float32 [2048, 2048], P('shard')
- grad_out: float32 [2048, 2048], P(None, 'shard')
- grad_gain_mlp: float32 [2048], P('shard')
- grad_gate: float32 [2048, 5632], P('shard')
- grad_up: float32 [2048, 5632], P('shard')
- grad_down: float32 [5632, 2048], P(None, 'shard')
All inputs are finite; a program needn't handle non-finite values.
Results may differ from a plain program's by a relative error of at most 0.017.
Values may be sent and summed in bfloat16 or wider, within the bound.
A program may use at most 384 MiB of HBM per device.

v0:
```python
import jax
import jax.numpy as jnp
from jax import lax
from jax.sharding import PartitionSpec as P

HEADS = 16
HD = 128
WIN = 256
CAP = 128
EPSILON = 1e-05
BF = jnp.bfloat16
F32 = jnp.float32


def mm(left, right):
    return jnp.dot(left, right, preferred_element_type=F32)


def mm_nt(left, right):
    return lax.dot_general(left, right, (((1,), (1,)), ((), ())), preferred_element_type=F32)


def mm_tn(left, right):
    return lax.dot_general(left, right, (((0,), (0,)), ((), ())), preferred_element_type=F32)


def swap(value, bit):
    size = lax.axis_size("rep")
    return lax.ppermute(value, "rep", [(i, i ^ bit) for i in range(size)])


def chip_bits():
    size, bits, bit = (lax.axis_size("rep"), [], 2)
    while bit < size:
        bits.append(bit)
        bit *= 2
    return bits


def chip_offsets():
    return list(range(0, lax.axis_size("rep"), 2))


def gather_chips(value):
    bits = chip_bits()
    if len(bits) == 2:
        one, two = bits
        half = value.shape[0] // 2
        by_one, by_two = (swap(value, one), swap(value, two))
        far = jnp.concatenate([swap(by_one[:half], two), swap(by_two[half:], one)], axis=0)
        return {0: value, one: by_one, two: by_two, one ^ two: far}
    blocks = {0: value}
    for bit in bits:
        blocks.update({d ^ bit: swap(b, bit) for d, b in list(blocks.items())})
    return blocks


def add(left, right):
    return left.astype(F32) + right.astype(F32)


def scatter_chips(blocks):
    bits = chip_bits()
    if len(bits) == 2:
        one, two = bits
        half = blocks[0].shape[0] // 2
        far = blocks[one ^ two]
        near_one, near_two = (blocks[one], blocks[two])
        top, bottom = (swap(far[:half], one), swap(far[half:], two))
        two_bottom, one_top = (swap(near_two[half:], two), swap(near_one[:half], one))
        two_top = swap(add(near_two[:half], top).astype(BF), two)
        one_bottom = swap(add(near_one[half:], bottom).astype(BF), one)
        by_one = jnp.concatenate([one_top, one_bottom], axis=0)
        by_two = jnp.concatenate([two_top, two_bottom], axis=0)
        return blocks[0].astype(F32) + by_one.astype(F32) + by_two.astype(F32)
    blocks = dict(blocks)
    for bit in reversed(bits):
        kept = {d: b for d, b in blocks.items() if not d & bit}
        blocks = {d: add(b, swap(blocks[d | bit], bit)).astype(BF) for d, b in kept.items()}
    return blocks[0].astype(F32)


def gather_plane(value):
    blocks = gather_chips(value)
    same = jnp.concatenate([blocks[d] for d in chip_offsets()], axis=0)
    return jnp.concatenate([same, swap(same, 1)], axis=0)


def scatter_plane(partial):
    half = partial.shape[0] // 2
    same = add(partial[:half], swap(partial[half:], 1)).astype(BF)
    offsets = chip_offsets()
    rows = half // len(offsets)
    return scatter_chips({d: same[i * rows : (i + 1) * rows] for i, d in enumerate(offsets)})


def rotary_tables(length):
    half = HD // 2
    positions = jnp.arange(length, dtype=F32)
    inverse = 10000.0 ** (-2.0 * jnp.arange(half, dtype=F32) / HD)
    angles = positions[:, None] * inverse[None, :]
    return (jnp.cos(angles)[:, None, :], jnp.sin(angles)[:, None, :])


def rotate(values, cos_table, sin_table):
    half = values.shape[-1] // 2
    first, second = (values[..., :half], values[..., half:])
    return jnp.concatenate(
        [first * cos_table - second * sin_table, second * cos_table + first * sin_table], axis=-1
    )


def plan_slots(route_ids, gate_values):
    hit_mask = route_ids == 0
    hit = jnp.any(hit_mask, axis=-1)
    weight = jnp.sum(jnp.where(hit_mask, gate_values, 0.0), axis=-1)
    ids = jnp.arange(route_ids.shape[0], dtype=jnp.int32)
    earlier = (ids[None, :] < ids[:, None]) & hit[None, :]
    order = jnp.sum(earlier.astype(jnp.int32), axis=1)
    kept = hit & (order < CAP)
    slots = jnp.arange(CAP, dtype=jnp.int32)
    table = (order[None, :] == slots[:, None]) & kept[None, :]
    return (table, jnp.where(kept, weight, 0.0))


def norm_back(grad_normed, source, root, gain):
    scaled = grad_normed * gain
    grad_gain = jnp.sum(grad_normed * source * root, axis=0)
    mean = jnp.mean(scaled * source, axis=-1, keepdims=True)
    return (grad_gain, root * scaled - source * (root * root * root) * mean)


def gather_vector(rows):
    size, me = (lax.axis_size("shard"), lax.axis_index("shard"))
    parts = [rows] + [
        lax.ppermute(rows, "shard", [(i, (i - k) % size) for i in range(size)])
        for k in range(1, size)
    ]
    twice = jnp.concatenate(parts + parts, axis=1)
    own = rows.shape[1]
    return lax.dynamic_slice_in_dim(twice, (size - me) % size * own, size * own, 1)


def attend(qkv, tables, allowed):
    rows = qkv.shape[0]
    length = allowed.shape[-1]
    seqs = rows // length
    width = qkv.shape[1] // 3
    heads = width // HD
    shape = (seqs, length, heads, HD)
    queries = rotate(qkv[:, :width].reshape(shape), *tables).astype(BF)
    keys = rotate(qkv[:, width : 2 * width].reshape(shape), *tables).astype(BF)
    values = qkv[:, 2 * width :].astype(BF).reshape(shape)
    scores = jnp.einsum("bqhd,bkhd->bhqk", queries, keys, preferred_element_type=F32) * HD ** (-0.5)
    scores = jnp.where(allowed[:, None], scores, -1e30)
    peak = jnp.max(scores, axis=-1, keepdims=True)
    raw = jnp.exp(scores - peak)
    total = jnp.sum(raw, axis=-1, keepdims=True)
    probs = (raw / total).astype(BF)
    context = jnp.einsum("bhqk,bkhd->bqhd", probs, values, preferred_element_type=F32).astype(BF)
    return (context.reshape(rows, width), (queries, keys, values, peak + jnp.log(total)))


def attend_back(saved, grad_context, tables, allowed):
    queries, keys, values, lse = saved
    shape = queries.shape
    grad_context = grad_context.reshape(shape)
    scale = HD ** (-0.5)
    scores = jnp.einsum("bqhd,bkhd->bhqk", queries, keys, preferred_element_type=F32) * scale
    scores = jnp.where(allowed[:, None], scores, -1e30)
    probs = jnp.exp(scores - lse)
    grad_values = jnp.einsum(
        "bhqk,bqhd->bkhd", probs.astype(BF), grad_context, preferred_element_type=F32
    ).astype(BF)
    grad_probs = jnp.einsum("bqhd,bkhd->bhqk", grad_context, values, preferred_element_type=F32)
    inner = jnp.sum(probs * grad_probs, axis=-1, keepdims=True)
    grad_scores = (probs * (grad_probs - inner)).astype(BF)
    grad_queries = (
        jnp.einsum("bhqk,bkhd->bqhd", grad_scores, keys, preferred_element_type=F32) * scale
    )
    grad_keys = (
        jnp.einsum("bhqk,bqhd->bkhd", grad_scores, queries, preferred_element_type=F32) * scale
    )
    cos_table, sin_table = tables
    rows = shape[0] * shape[1]
    return jnp.concatenate(
        [
            rotate(grad_queries, cos_table, -sin_table).astype(BF).reshape(rows, -1),
            rotate(grad_keys, cos_table, -sin_table).astype(BF).reshape(rows, -1),
            grad_values.reshape(rows, -1),
        ],
        axis=1,
    )


def per_device(
    layer_input,
    gain_attn,
    w_query,
    w_key,
    w_value,
    w_out,
    gain_mlp,
    w_gate,
    w_up,
    w_down,
    segments,
    attn_route,
    attn_gate,
    mlp_route,
    mlp_gate,
    cotangent,
):
    length = layer_input.shape[0]
    size = lax.axis_size("rep")
    me = lax.axis_index("rep")
    block = w_query.shape[1] // size
    hidden_block = w_gate.shape[1] // size
    offsets = chip_offsets()

    def columns(weight, width):
        return lax.dynamic_slice_in_dim(weight, me * width, width, 1)

    def rows_of(weight, height):
        return lax.dynamic_slice_in_dim(weight, me * height, height, 0)

    own_qkv = jnp.concatenate([columns(w, block) for w in (w_query, w_key, w_value)], axis=1)
    own_qkv = lax.all_gather(own_qkv, "shard", axis=0, tiled=True)
    own_out = lax.all_gather(rows_of(w_out, block), "shard", axis=1, tiled=True)
    qkv_w = gather_chips(own_qkv)
    out_w = gather_chips(own_out)
    gate_up = jnp.concatenate([columns(w_gate, hidden_block), columns(w_up, hidden_block)], axis=1)
    gate_up = lax.all_gather(gate_up, "shard", axis=0, tiled=True)
    down = lax.all_gather(rows_of(w_down, hidden_block), "shard", axis=1, tiled=True)
    gains = gather_vector(jnp.stack([gain_attn, gain_mlp])).astype(F32)
    gain_one, gain_two = (gains[0], gains[1])
    table, mix = plan_slots(mlp_route, mlp_gate)
    pick = table.astype(BF)
    upstream = cotangent.astype(F32)
    slot_weight = jnp.sum(jnp.where(table, mix[None, :], 0.0), axis=1)[:, None]
    slot_grad = (mm(pick, cotangent) * slot_weight).astype(BF)
    all_slot_grad = gather_plane(slot_grad)
    inputs = layer_input.astype(F32)
    root_one = lax.rsqrt(jnp.mean(inputs * inputs, axis=-1, keepdims=True) + EPSILON)
    normed = (inputs * root_one * gain_one).astype(BF)
    both = jnp.concatenate([normed, swap(normed, 1)], axis=0)
    seg = jnp.concatenate([segments, swap(segments, 1)], axis=0)
    ids = jnp.arange(length, dtype=jnp.int32)
    distance = ids[:, None] - ids[None, :]
    near = (distance >= 0) & (distance < WIN)
    allowed = (seg[:, :, None] == seg[:, None, :]) & near[None]
    tables = rotary_tables(length)
    context, saved = ({}, {})
    for d in offsets:
        context[d], saved[d] = attend(mm(both, qkv_w[d]), tables, allowed)
    all_context = jnp.concatenate([context[d] for d in offsets], axis=1)
    all_out = jnp.concatenate([out_w[d] for d in offsets], axis=0)
    projected = mm(all_context, all_out)
    projected = projected[:length] + swap(projected[length:].astype(BF), 1).astype(F32)
    attn_weight = jnp.sum(jnp.where(attn_route == 0, attn_gate, 0.0), axis=-1)[:, None]
    hidden = inputs + projected * attn_weight
    root_two = lax.rsqrt(jnp.mean(hidden * hidden, axis=-1, keepdims=True) + EPSILON)
    normed_two = (hidden * root_two * gain_two).astype(BF)
    dispatched = gather_plane(mm(pick, normed_two).astype(BF))
    act = mm(dispatched, gate_up)
    gate_act, up_act = (act[:, :hidden_block], act[:, hidden_block:])
    sigmoid = jax.nn.sigmoid(gate_act)
    silu = gate_act * sigmoid
    inner = (silu * up_act).astype(BF)
    grad_inner = mm_nt(all_slot_grad, down)
    grad_gate_act = (grad_inner * up_act * sigmoid * (1.0 + gate_act * (1.0 - sigmoid))).astype(BF)
    grad_up_act = (grad_inner * silu).astype(BF)
    grad_act = jnp.concatenate([grad_gate_act, grad_up_act], axis=1)
    grad_disp = scatter_plane(mm_nt(grad_act, gate_up).astype(BF)).astype(BF)
    expert_out = scatter_plane(mm(inner, down).astype(BF)).astype(BF)
    output = (hidden + mm_tn(pick, expert_out) * mix[:, None]).astype(BF)
    grad_gate_up = mm_tn(dispatched, grad_act).astype(BF)
    grad_down = mm_tn(inner, all_slot_grad).astype(BF)
    grad_normed_two = mm_tn(pick, grad_disp)
    grad_gain_two, through = norm_back(grad_normed_two, hidden, root_two, gain_two)
    grad_hidden = upstream + through
    grad_projected = (grad_hidden * attn_weight).astype(BF)
    both_grad = jnp.concatenate([grad_projected, swap(grad_projected, 1)], axis=0)
    grad_out_w = mm_tn(all_context, both_grad).astype(BF)
    grad_context = mm_nt(both_grad, all_out).astype(BF)
    grad_lin = {
        d: attend_back(saved[d], grad_context[:, i * block : (i + 1) * block], tables, allowed)
        for i, d in enumerate(offsets)
    }
    grad_qkv_w = {d: mm_tn(both, grad_lin[d]).astype(BF) for d in offsets}
    grad_normed = sum((mm_nt(grad_lin[d], qkv_w[d]) for d in offsets))
    grad_normed = grad_normed[:length] + swap(grad_normed[length:].astype(BF), 1).astype(F32)
    grad_gain_one, first = norm_back(grad_normed, inputs, root_one, gain_one)
    grad_input = (grad_hidden + first).astype(BF)

    def spread(value, axis):
        return lax.all_gather(value, "rep", axis=axis, tiled=True).astype(F32)

    sum_gu = lax.psum_scatter(grad_gate_up, "shard", scatter_dimension=0, tiled=True)
    sum_down = lax.psum_scatter(grad_down, "shard", scatter_dimension=1, tiled=True)
    own_grad_out = scatter_chips(
        {d: grad_out_w[i * block : (i + 1) * block] for i, d in enumerate(offsets)}
    ).astype(BF)
    sum_out = lax.psum_scatter(own_grad_out, "shard", scatter_dimension=1, tiled=True)
    own_grad_qkv = scatter_chips(grad_qkv_w).astype(BF)
    sum_qkv = lax.psum_scatter(own_grad_qkv, "shard", scatter_dimension=0, tiled=True)
    grad_gate = spread(sum_gu[:, :hidden_block], 1)
    grad_up = spread(sum_gu[:, hidden_block:], 1)
    grad_down = spread(sum_down, 0)
    grad_out = spread(sum_out, 0)
    grad_query, grad_key, grad_value = (
        spread(sum_qkv[:, i * block : (i + 1) * block], 1) for i in range(3)
    )
    gain_grads = lax.psum(jnp.stack([grad_gain_one, grad_gain_two]), ("rep", "shard"))
    own = gain_attn.shape[0]
    gain_grads = lax.dynamic_slice_in_dim(gain_grads, lax.axis_index("shard") * own, own, 1)
    return (
        output,
        grad_input,
        gain_grads[0],
        grad_query,
        grad_key,
        grad_value,
        grad_out,
        gain_grads[1],
        grad_gate,
        grad_up,
        grad_down,
    )


def solution(mesh):
    tokens = P(("rep", "shard"), None)
    tall, wide, vector = (P("shard", None), P(None, "shard"), P("shard"))
    weights = (vector, tall, tall, tall, wide, vector, tall, tall, wide)
    return jax.shard_map(
        per_device,
        mesh=mesh,
        in_specs=(tokens, *weights) + (tokens,) * 6,
        out_specs=(tokens, tokens, *weights),
        check_vma=False,
    )
```

profile of v0, /device:TPU:0, one launch (start us, length us, event | category | flops | bytes accessed | tf_op | source)
XLA Modules:
  0.0 1188.0 jit_solution(6927684167405556137)
XLA Ops:
  25.8 15.1 %all-gather.14.cloned.1.call-done = bf16[256,2048]{1,0:T(8,128)(2,1)} async-done(((bf16[256,512]{1,0:T(8,128)(2,1)}), bf16[256,2048]{1,0:T(8,128)(2,1)}) %all-gather.14.cloned.1.call-update) | async-done | bytes 1048592 | tf_op jit(solution)/shard_map/all_gather | solution.py:229
  48.7 57.4 %all-gather.12.cloned.1.call-done = bf16[2048,768]{1,0:T(8,128)(2,1)} async-done(((bf16[512,768]{1,0:T(8,128)(2,1)}), bf16[2048,768]{1,0:T(8,128)(2,1)}) %all-gather.12.cloned.1.call-update) | async-done | bytes 3145744 | tf_op jit(solution)/shard_map/all_gather | solution.py:228
  124.0 63.3 %collective-permute-done.12 = bf16[128,2048]{1,0:T(8,128)(2,1)S(1)} collective-permute-done((bf16[128,2048]{1,0:T(8,128)(2,1)S(1)}, bf16[128,2048]{1,0:T(8,128)(2,1)S(1)}, u32[]{:S(2)}, u32[]{:S(2)}) %collective-permute-start.12) | collective-permute-done | bytes 524320 | tf_op jit(solution)/shard_map/ppermute | solution.py:29
  221.0 8.6 fusion.149
  342.6 11.5 collective-permute-done.26
  364.9 8.4 collective-permute-done.14
  389.3 12.3 %fusion.178 = f32[1024,1408]{1,0:T(8,128)} fusion(bf16[1024,2048]{1,0:T(8,128)(2,1)} %constant_dynamic-update-slice_fusion.20, bf16[2048,1408]{1,0:T(8,128)(2,1)} %all-gather.16.cloned.1.call-done), kind=kOutput, calls=%fused_computation.378 | convolution fusion | flops 5905580032 | bytes 15728640 | tf_op jit(solution)/shard_map/dot_general | solution.py:16
  401.6 40.2 %all-gather.18.cloned.1.call-done = bf16[704,2048]{1,0:T(8,128)(2,1)} async-done(((bf16[704,512]{1,0:T(8,128)(2,1)}), bf16[704,2048]{1,0:T(8,128)(2,1)}) %all-gather.18.cloned.1.call-update) | async-done | bytes 2883600 | tf_op jit(solution)/shard_map/all_gather | solution.py:234
  441.8 10.3 multiply_convert_fusion.7
  505.1 10.7 collective-permute-done.49
  527.7 9.9 collective-permute-done.48
  539.5 7.6 convolution_convert_fusion.8
  626.2 8.0 convolution_convert_fusion.6
  650.6 10.1 collective-permute-done.41
  673.1 22.7 %collective-permute-done.40 = bf16[1024,768]{1,0:T(8,128)(2,1)} collective-permute-done((bf16[1024,768]{1,0:T(8,128)(2,1)}, bf16[1024,768]{1,0:T(8,128)(2,1)}, u32[]{:S(2)}, u32[]{:S(2)}) %collective-permute-start.40) | collective-permute-done | bytes 1572896 | tf_op jit(solution)/shard_map/ppermute | solution.py:29
  695.8 31.6 %collective-permute-done.42 = bf16[1024,768]{1,0:T(8,128)(2,1)} collective-permute-done((bf16[1024,768]{1,0:T(8,128)(2,1)}, bf16[1024,768]{1,0:T(8,128)(2,1)}, u32[]{:S(2)}, u32[]{:S(2)}) %collective-permute-start.42) | collective-permute-done | bytes 1572896 | tf_op jit(solution)/shard_map/ppermute | solution.py:29
  727.4 9.3 add_convert_fusion
  736.9 10.9 convolution_convert_fusion
  749.2 46.1 %reduce-scatter.5.cloned.1.call-done = bf16[512,768]{1,0:T(8,128)(2,1)} async-done(((bf16[2048,768]{1,0:T(8,128)(2,1)}), bf16[512,768]{1,0:T(8,128)(2,1)}) %reduce-scatter.5.cloned.1.call-update) | async-done | bytes 786448 | tf_op jit(solution)/shard_map/reduce_scatter | solution.py:306
  798.7 101.9 %reduce-scatter.9.cloned.1.call-done = bf16[512,1408]{1,0:T(8,128)(2,1)} async-done(((bf16[2048,1408]{1,0:T(8,128)(2,1)}), bf16[512,1408]{1,0:T(8,128)(2,1)}) %reduce-scatter.9.cloned.1.call-update) | async-done | bytes 1441808 | tf_op jit(solution)/shard_map/reduce_scatter | solution.py:299
  914.4 7.8 fusion.181
  922.2 7.7 fusion.179
  929.9 7.7 fusion.180
  937.6 11.8 add_add_fusion
  962.2 10.7 collective-permute-done.23
  1000.2 39.9 %psum.7 = f32[2,2048]{1,0:T(2,128)S(1)} all-reduce(f32[2,2048]{1,0:T(2,128)S(1)} %pad_maximum_fusion.43), channel_id=1, replica_groups=mesh['rep'=8,'shard'=4] {'rep','shard'}, use_global_device_ids=true, to_apply=%region_23.24 | all-reduce | flops 4096 | bytes 32768 | tf_op jit(solution)/shard_map/psum | solution.py:314
  1051.2 8.7 convert_element_type.490
  1068.2 13.3 %all-gather.24.cloned.1.call-done = bf16[512,2048]{1,0:T(8,128)(2,1)} async-done(((bf16[512,256]{1,0:T(8,128)(2,1)}), bf16[512,2048]{1,0:T(8,128)(2,1)}) %all-gather.24.cloned.1.call-update) | async-done | bytes 2097168 | tf_op jit(solution)/shard_map/all_gather | solution.py:297
  1085.6 41.1 %all-gather.28.cloned.1.call-done = bf16[512,5632]{0,1:T(8,128)(2,1)} async-done(((bf16[512,704]{0,1:T(8,128)(2,1)}), bf16[512,5632]{0,1:T(8,128)(2,1)}) %all-gather.28.cloned.1.call-update) | async-done | bytes 5767184 | tf_op jit(solution)/shard_map/all_gather | solution.py:297
  1126.8 9.1 copy.333
  1135.8 36.2 %all-gather.30.cloned.1.call-done = bf16[512,5632]{0,1:T(8,128)(2,1)} async-done(((bf16[512,704]{0,1:T(8,128)(2,1)}), bf16[512,5632]{0,1:T(8,128)(2,1)}) %all-gather.30.cloned.1.call-update) | async-done | bytes 5767184 | tf_op jit(solution)/shard_map/all_gather | solution.py:297
  1172.0 9.2 copy.334
  (633 shorter events, 472.7 us)
Async XLA Ops:
  7.2 33.6 %all-gather.14.cloned.1.call-start = ((), (), s32[]{:S(2)}) async-start(), calls=%async_computation.5 | async-start | bytes 1310720 | tf_op jit(solution)/shard_map/all_gather | solution.py:229
  9.5 96.5 %all-gather.12.cloned.1.call-start = ((), (), s32[]{:S(2)}) async-start(), calls=%async_computation.4 | async-start | bytes 3932160 | tf_op jit(solution)/shard_map/all_gather | solution.py:228
  12.7 376.6 %all-gather.16.cloned.1.call-start = ((), (), s32[]{:S(2)}) async-start(), calls=%async_computation.6 | async-start | bytes 7208960 | tf_op jit(solution)/shard_map/all_gather | solution.py:233
  18.9 88.6 %collective-permute-start.4 = (s32[1,512]{1,0:T(1,128)S(1)}, s32[1,512]{1,0:T(1,128)S(1)}, u32[]{:S(2)}, u32[]{:S(2)}) collective-permute-start(s32[1,512]{1,0:T(1,128)S(1)} %copy-done.131), channel_id=1, source_target_pairs={{0,4},{4,0},{8,12},{12,8},{16,20},{20,16},{24,28},{28,24},{1,5},{5... | collective-permute-start | bytes 6152 | tf_op jit(solution)/shard_map/ppermute | solution.py:29
  25.4 164.0 %collective-permute-start.3 = (bf16[512,2048]{1,0:T(8,128)(2,1)}, bf16[512,2048]{1,0:T(8,128)(2,1)}, u32[]{:S(2)}, u32[]{:S(2)}) collective-permute-start(bf16[512,2048]{1,0:T(8,128)(2,1)} %fusion.2), channel_id=1, source_target_pairs={{0,4},{4,0},{8,12},{12,8},{16,20},{20,16},{24,28},{28,24},{1,5},{5... | collective-permute-start | bytes 6291464 | tf_op jit(solution)/shard_map/ppermute | solution.py:29
  40.9 67.1 %collective-permute-start.9 = (bf16[256,2048]{1,0:T(8,128)(2,1)}, bf16[256,2048]{1,0:T(8,128)(2,1)}, u32[]{:S(2)}, u32[]{:S(2)}) collective-permute-start(bf16[256,2048]{1,0:T(8,128)(2,1)} %all-gather.14.cloned.1.call-done), channel_id=1, source_target_pairs={{0,8},{4,12},{8,0},{12,4},{16,24},{20,28},{24,16},{28,20},{1,9},{5... | collective-permute-start | bytes 3145736 | tf_op jit(solution)/shard_map/ppermute | solution.py:29
  45.0 396.7 %all-gather.18.cloned.1.call-start = ((), (), s32[]{:S(2)}) async-start(), calls=%async_computation.7 | async-start | bytes 3604480 | tf_op jit(solution)/shard_map/all_gather | solution.py:234
  45.1 66.8 %collective-permute-start.10 = (bf16[256,2048]{1,0:T(8,128)(2,1)}, bf16[256,2048]{1,0:T(8,128)(2,1)}, u32[]{:S(2)}, u32[]{:S(2)}) collective-permute-start(bf16[256,2048]{1,0:T(8,128)(2,1)} %all-gather.14.cloned.1.call-done), channel_id=1, source_target_pairs={{0,16},{4,20},{8,24},{12,28},{16,0},{20,4},{24,8},{28,12},{1,17},{... | collective-permute-start | bytes 3145736 | tf_op jit(solution)/shard_map/ppermute | solution.py:29
  106.0 104.2 %collective-permute-start.5 = (bf16[2048,768]{1,0:T(8,128)(2,1)}, bf16[2048,768]{1,0:T(8,128)(2,1)}, u32[]{:S(2)}, u32[]{:S(2)}) collective-permute-start(bf16[2048,768]{1,0:T(8,128)(2,1)} %all-gather.12.cloned.1.call-done), channel_id=1, source_target_pairs={{0,8},{4,12},{8,0},{12,4},{16,24},{20,28},{24,16},{28,20},{1,9},{5... | collective-permute-start | bytes 9437192 | tf_op jit(solution)/shard_map/ppermute | solution.py:29
  113.0 74.2 %collective-permute-start.12 = (bf16[128,2048]{1,0:T(8,128)(2,1)S(1)}, bf16[128,2048]{1,0:T(8,128)(2,1)S(1)}, u32[]{:S(2)}, u32[]{:S(2)}) collective-permute-start(bf16[128,2048]{1,0:T(8,128)(2,1)S(1)} %slice.473), channel_id=1, source_target_pairs={{0,8},{4,12},{8,0},{12,4},{16,24},{20,28},{24,16},{28,20},{1,9},{5... | collective-permute-start | bytes 1572872 | tf_op jit(solution)/shard_map/ppermute | solution.py:29
  115.0 106.0 %collective-permute-start.6 = (bf16[2048,768]{1,0:T(8,128)(2,1)}, bf16[2048,768]{1,0:T(8,128)(2,1)}, u32[]{:S(2)}, u32[]{:S(2)}) collective-permute-start(bf16[2048,768]{1,0:T(8,128)(2,1)} %all-gather.12.cloned.1.call-done), channel_id=1, source_target_pairs={{0,16},{4,20},{8,24},{12,28},{16,0},{20,4},{24,8},{28,12},{1,17},{... | collective-permute-start | bytes 9437192 | tf_op jit(solution)/shard_map/ppermute | solution.py:29
  212.9 52.7 %collective-permute-start.7 = (bf16[1024,768]{1,0:T(8,128)(2,1)}, bf16[1024,768]{1,0:T(8,128)(2,1)}, u32[]{:S(2)}, u32[]{:S(2)}) collective-permute-start(bf16[1024,768]{1,0:T(8,128)(2,1)} %slice.463), channel_id=1, source_target_pairs={{0,16},{4,20},{8,24},{12,28},{16,0},{20,4},{24,8},{28,12},{1,17},{... | collective-permute-start | bytes 4718600 | tf_op jit(solution)/shard_map/ppermute | solution.py:29
  233.8 35.3 %collective-permute-start.8 = (bf16[1024,768]{1,0:T(8,128)(2,1)}, bf16[1024,768]{1,0:T(8,128)(2,1)}, u32[]{:S(2)}, u32[]{:S(2)}) collective-permute-start(bf16[1024,768]{1,0:T(8,128)(2,1)} %slice.464), channel_id=1, source_target_pairs={{0,8},{4,12},{8,0},{12,4},{16,24},{20,28},{24,16},{28,20},{1,9},{5... | collective-permute-start | bytes 4718600 | tf_op jit(solution)/shard_map/ppermute | solution.py:29
  383.7 364.2 %reduce-scatter.7.cloned.1.call-start = ((), (), s32[]{:S(2)}) async-start(), calls=%async_computation.12 | async-start | bytes 1310720 | tf_op jit(solution)/shard_map/reduce_scatter | solution.py:304
  539.3 209.3 %reduce-scatter.11.cloned.1.call-start = ((), (), s32[]{:S(2)}) async-start(), calls=%async_computation.17 | async-start | bytes 3604480 | tf_op jit(solution)/shard_map/reduce_scatter | solution.py:300
  547.1 248.2 %reduce-scatter.5.cloned.1.call-start = ((), (), s32[]{:S(2)}) async-start(), calls=%async_computation.8 | async-start | bytes 3932160 | tf_op jit(solution)/shard_map/reduce_scatter | solution.py:306
  623.0 37.6 %collective-permute-start.41 = (bf16[1024,768]{1,0:T(8,128)(2,1)}, bf16[1024,768]{1,0:T(8,128)(2,1)}, u32[]{:S(2)}, u32[]{:S(2)}) collective-permute-start(bf16[1024,768]{1,0:T(8,128)(2,1)} %get-tuple-element.55), channel_id=1, source_target_pairs={{0,16},{4,20},{8,24},{12,28},{16,0},{20,4},{24,8},{28,12},{1,17},{... | collective-permute-start | bytes 4718600 | tf_op jit(solution)/shard_map/ppermute | solution.py:29
  624.5 40.8 %collective-permute-start.43 = (bf16[1024,768]{1,0:T(8,128)(2,1)}, bf16[1024,768]{1,0:T(8,128)(2,1)}, u32[]{:S(2)}, u32[]{:S(2)}) collective-permute-start(bf16[1024,768]{1,0:T(8,128)(2,1)} %get-tuple-element.54), channel_id=1, source_target_pairs={{0,8},{4,12},{8,0},{12,4},{16,24},{20,28},{24,16},{28,20},{1,9},{5... | collective-permute-start | bytes 4718600 | tf_op jit(solution)/shard_map/ppermute | solution.py:29
  640.3 55.5 %collective-permute-start.40 = (bf16[1024,768]{1,0:T(8,128)(2,1)}, bf16[1024,768]{1,0:T(8,128)(2,1)}, u32[]{:S(2)}, u32[]{:S(2)}) collective-permute-start(bf16[1024,768]{1,0:T(8,128)(2,1)} %slice.523), channel_id=1, source_target_pairs={{0,8},{4,12},{8,0},{12,4},{16,24},{20,28},{24,16},{28,20},{1,9},{5... | collective-permute-start | bytes 4718600 | tf_op jit(solution)/shard_map/ppermute | solution.py:29
  650.0 45.8 %collective-permute-start.45 = (bf16[1024,768]{1,0:T(8,128)(2,1)}, bf16[1024,768]{1,0:T(8,128)(2,1)}, u32[]{:S(2)}, u32[]{:S(2)}) collective-permute-start(bf16[1024,768]{1,0:T(8,128)(2,1)} %slice.528), channel_id=1, source_target_pairs={{0,16},{4,20},{8,24},{12,28},{16,0},{20,4},{24,8},{28,12},{1,17},{... | collective-permute-start | bytes 4718600 | tf_op jit(solution)/shard_map/ppermute | solution.py:29
  663.7 63.7 %collective-permute-start.42 = (bf16[1024,768]{1,0:T(8,128)(2,1)}, bf16[1024,768]{1,0:T(8,128)(2,1)}, u32[]{:S(2)}, u32[]{:S(2)}) collective-permute-start(bf16[1024,768]{1,0:T(8,128)(2,1)} %add_convert_fusion.5), channel_id=1, source_target_pairs={{0,8},{4,12},{8,0},{12,4},{16,24},{20,28},{24,16},{28,20},{1,9},{5... | collective-permute-start | bytes 4718600 | tf_op jit(solution)/shard_map/ppermute | solution.py:29
  668.4 59.1 %collective-permute-start.44 = (bf16[1024,768]{1,0:T(8,128)(2,1)}, bf16[1024,768]{1,0:T(8,128)(2,1)}, u32[]{:S(2)}, u32[]{:S(2)}) collective-permute-start(bf16[1024,768]{1,0:T(8,128)(2,1)} %add_convert_fusion.4), channel_id=1, source_target_pairs={{0,16},{4,20},{8,24},{12,28},{16,0},{20,4},{24,8},{28,12},{1,17},{... | collective-permute-start | bytes 4718600 | tf_op jit(solution)/shard_map/ppermute | solution.py:29
  736.8 163.8 %reduce-scatter.9.cloned.1.call-start = ((), (), s32[]{:S(2)}) async-start(), calls=%async_computation.14 | async-start | bytes 7208960 | tf_op jit(solution)/shard_map/reduce_scatter | solution.py:299
  747.8 299.1 %all-gather.26.cloned.1.call-start = ((), (), s32[]{:S(2)}) async-start(), calls=%async_computation.13 | async-start | bytes 2359296 | tf_op jit(solution)/shard_map/all_gather | solution.py:297
  748.6 302.6 %all-gather.32.cloned.1.call-start = ((), (), s32[]{:S(2)}) async-start(), calls=%async_computation.18 | async-start | bytes 6488064 | tf_op jit(solution)/shard_map/all_gather | solution.py:297
  749.1 310.7 %all-gather.20.cloned.1.call-start = ((), (), s32[]{:S(2)}) async-start(), calls=%async_computation.9 | async-start | bytes 2359296 | tf_op jit(solution)/shard_map/all_gather | solution.py:297
  797.3 266.8 %all-gather.22.cloned.1.call-start = ((), (), s32[]{:S(2)}) async-start(), calls=%async_computation.10 | async-start | bytes 2359296 | tf_op jit(solution)/shard_map/all_gather | solution.py:297
  797.9 283.6 %all-gather.24.cloned.1.call-start = ((), (), s32[]{:S(2)}) async-start(), calls=%async_computation.11 | async-start | bytes 2359296 | tf_op jit(solution)/shard_map/all_gather | solution.py:297
  798.7 328.1 %all-gather.28.cloned.1.call-start = ((), (), s32[]{:S(2)}) async-start(), calls=%async_computation.15 | async-start | bytes 6488064 | tf_op jit(solution)/shard_map/all_gather | solution.py:297
  903.6 268.4 %all-gather.30.cloned.1.call-start = ((), (), s32[]{:S(2)}) async-start(), calls=%async_computation.16 | async-start | bytes 6488064 | tf_op jit(solution)/shard_map/all_gather | solution.py:297
  914.1 37.1 %collective-permute-start.19 = (bf16[512,2048]{1,0:T(8,128)(2,1)}, bf16[512,2048]{1,0:T(8,128)(2,1)}, u32[]{:S(2)}, u32[]{:S(2)}) collective-permute-start(bf16[512,2048]{1,0:T(8,128)(2,1)} %slice.482), channel_id=1, source_target_pairs={{0,4},{4,0},{8,12},{12,8},{16,20},{20,16},{24,28},{28,24},{1,5},{5... | collective-permute-start | bytes 6291464 | tf_op jit(solution)/shard_map/ppermute | solution.py:29
  951.0 44.8 %collective-permute-start.39 = (bf16[512,2048]{1,0:T(8,128)(2,1)}, bf16[512,2048]{1,0:T(8,128)(2,1)}, u32[]{:S(2)}, u32[]{:S(2)}) collective-permute-start(bf16[512,2048]{1,0:T(8,128)(2,1)} %slice.618), channel_id=1, source_target_pairs={{0,4},{4,0},{8,12},{12,8},{16,20},{20,16},{24,28},{28,24},{1,5},{5... | collective-permute-start | bytes 6291464 | tf_op jit(solution)/shard_map/ppermute | solution.py:29
  (174 other events, 2055.3 us)
Sparse Core Ops, SparseCore 0:
  10.2 30.6 all-gather.13
  43.0 62.9 all-gather.11
  107.6 105.3 all-gather.15
  383.8 57.9 all-gather.17
  539.5 25.8 reduce-scatter.6
  567.6 54.8 reduce-scatter.10
  736.9 58.3 reduce-scatter.4
  798.3 102.2 reduce-scatter.8
  902.6 28.3 all-gather.25
  933.0 56.7 all-gather.31
  991.8 29.1 all-gather.19
  1022.8 28.3 all-gather.21
  1053.3 28.1 all-gather.23
  1083.4 43.3 all-gather.27
  1128.6 43.3 all-gather.29
where the time goes:
time: 1190 us
  waiting for transfers between devices  592 us (50%)
  matrix products  222 us (19%)
  local copies, waits for them, and re-layouts  180 us (15%)
  other arithmetic  85.9 us (7%)
  starting transfers between devices  52.3 us (4%)
  blocking collectives  39.9 us (3%)
  between operations  16.3 us (1%)
    ppermute x49, waiting for transfers between devices, swap(): return lax.ppermute(value, 'rep', [(i, i ^ bit) for i in range(size)])  238 us
    reduce_scatter x1, waiting for transfers between devices, per_device(): lax.psum_scatter(grad_gate_up, 'shard', scatter_dimension=0, tiled=True)  102 us
    all_gather x7, waiting for transfers between devices, spread(): return lax.all_gather(value, 'rep', axis=axis, tiled=True).astype(F32)  90.6 us
    dot_general x9, matrix products, mm_tn(): lax.dot_general(left, right, (((0,), (0,)), ((), ())), preferred_element_...  59.7 us
    dot_general x7, matrix products, mm_nt(): lax.dot_general(left, right, (((1,), (1,)), ((), ())), preferred_element_...  59.5 us
    all_gather x1, waiting for transfers between devices, per_device(): own_qkv = lax.all_gather(own_qkv, 'shard', axis=0, tiled=True)  57.4 us
    dot_general x9, matrix products, mm(): return jnp.dot(left, right, preferred_element_type=F32)  54.5 us
    unnamed x308, local copies, waits for them, and re-layouts  49.1 us
  transfers between devices with their start and end apart: 67, of which 40 were waited for; matrix products, arithmetic and copies ran while one was open for 36% of the time, Pallas kernels for 0%

commit v1 on v0

--- a/solution.py
+++ b/solution.py
@@ -311,7 +311,9 @@
     grad_query, grad_key, grad_value = (
         spread(sum_qkv[:, i * block : (i + 1) * block], 1) for i in range(3)
     )
-    gain_grads = lax.psum(jnp.stack([grad_gain_one, grad_gain_two]), ("rep", "shard"))
+    gain_grads = jnp.sum(
+        lax.all_gather(jnp.stack([grad_gain_one, grad_gain_two]), ("rep", "shard")), axis=0
+    )
     own = gain_attn.shape[0]
     gain_grads = lax.dynamic_slice_in_dim(gain_grads, lax.axis_index("shard") * own, own, 1)
     return (

time: 1190 us -> 1190 us (level)
  waiting for transfers between devices: 592 us -> 560 us
  blocking collectives: 39.9 us -> 71.6 us
    all_gather x0 -> x1, blocking collectives: none -> 71.6 us  [per_device(): lax.all_gather(jnp.stack([grad_gain_one, grad_gain_two]), ('rep', 'shard'))]
    psum x1 -> x0, blocking collectives: 39.9 us -> none  [per_device(): lax.psum(jnp.stack([grad_gain_one, grad_gain_two]), ('rep', 'shard'))]
    all_gather x7, waiting for transfers between devices: 90.6 us -> 58.7 us  [spread(): return lax.all_gather(value, 'rep', axis=axis, tiled=True).astype(F32)]
  transfers between devices with their start and end apart: 67 -> 67, of which waited for: 40 -> 39; matrix products, arithmetic and copies ran while one was open for 36% -> 36% of each run, Pallas kernels for 0% -> 0%
where the time goes in v1:
time: 1190 us
  waiting for transfers between devices  560 us (47%)
  matrix products  222 us (19%)
  local copies, waits for them, and re-layouts  180 us (15%)
  other arithmetic  86 us (7%)
  blocking collectives  71.6 us (6%)
  starting transfers between devices  52.3 us (4%)
  between operations  16.3 us (1%)
    ppermute x49, waiting for transfers between devices, swap(): return lax.ppermute(value, 'rep', [(i, i ^ bit) for i in range(size)])  238 us
    reduce_scatter x1, waiting for transfers between devices, per_device(): lax.psum_scatter(grad_gate_up, 'shard', scatter_dimension=0, tiled=True)  102 us
    all_gather x1, blocking collectives, per_device(): lax.all_gather(jnp.stack([grad_gain_one, grad_gain_two]), ('rep', 'shard'))  71.6 us
    dot_general x9, matrix products, mm_tn(): lax.dot_general(left, right, (((0,), (0,)), ((), ())), preferred_element_...  59.7 us
    dot_general x7, matrix products, mm_nt(): lax.dot_general(left, right, (((1,), (1,)), ((), ())), preferred_element_...  59.5 us
    all_gather x7, waiting for transfers between devices, spread(): return lax.all_gather(value, 'rep', axis=axis, tiled=True).astype(F32)  58.7 us
    all_gather x1, waiting for transfers between devices, per_device(): own_qkv = lax.all_gather(own_qkv, 'shard', axis=0, tiled=True)  57.4 us
    dot_general x9, matrix products, mm(): return jnp.dot(left, right, preferred_element_type=F32)  54.5 us
  transfers between devices with their start and end apart: 67, of which 39 were waited for; matrix products, arithmetic and copies ran while one was open for 36% of the time, Pallas kernels for 0%

profile of v1, /device:TPU:0, one launch (start us, length us, event | category | flops | bytes accessed | tf_op | source)
XLA Modules:
  0.0 1188.0 jit_solution(11623226232861256016)
XLA Ops:
  25.8 15.1 %all-gather.16.cloned.1.call-done = bf16[256,2048]{1,0:T(8,128)(2,1)} async-done(((bf16[256,512]{1,0:T(8,128)(2,1)}), bf16[256,2048]{1,0:T(8,128)(2,1)}) %all-gather.16.cloned.1.call-update) | async-done | bytes 1048592 | tf_op jit(solution)/shard_map/all_gather | solution.py:229
  48.7 57.4 %all-gather.14.cloned.1.call-done = bf16[2048,768]{1,0:T(8,128)(2,1)} async-done(((bf16[512,768]{1,0:T(8,128)(2,1)}), bf16[2048,768]{1,0:T(8,128)(2,1)}) %all-gather.14.cloned.1.call-update) | async-done | bytes 3145744 | tf_op jit(solution)/shard_map/all_gather | solution.py:228
  124.0 63.3 %collective-permute-done.12 = bf16[128,2048]{1,0:T(8,128)(2,1)S(1)} collective-permute-done((bf16[128,2048]{1,0:T(8,128)(2,1)S(1)}, bf16[128,2048]{1,0:T(8,128)(2,1)S(1)}, u32[]{:S(2)}, u32[]{:S(2)}) %collective-permute-start.12) | collective-permute-done | bytes 524320 | tf_op jit(solution)/shard_map/ppermute | solution.py:29
  221.0 8.6 fusion.149
  292.3 7.5 subtract_convert_fusion.9
  342.6 11.5 collective-permute-done.26
  364.9 8.4 collective-permute-done.14
  389.3 12.3 %fusion.178 = f32[1024,1408]{1,0:T(8,128)} fusion(bf16[1024,2048]{1,0:T(8,128)(2,1)} %constant_dynamic-update-slice_fusion.20, bf16[2048,1408]{1,0:T(8,128)(2,1)} %all-gather.18.cloned.1.call-done), kind=kOutput, calls=%fused_computation.378 | convolution fusion | flops 5905580032 | bytes 15728640 | tf_op jit(solution)/shard_map/dot_general | solution.py:16
  401.6 40.2 %all-gather.20.cloned.1.call-done = bf16[704,2048]{1,0:T(8,128)(2,1)} async-done(((bf16[704,512]{1,0:T(8,128)(2,1)}), bf16[704,2048]{1,0:T(8,128)(2,1)}) %all-gather.20.cloned.1.call-update) | async-done | bytes 2883600 | tf_op jit(solution)/shard_map/all_gather | solution.py:234
  441.8 10.3 multiply_convert_fusion.7
  505.1 10.7 collective-permute-done.49
  527.7 9.9 collective-permute-done.48
  539.5 7.6 convolution_convert_fusion.8
  626.2 8.0 convolution_convert_fusion.6
  650.6 10.1 collective-permute-done.41
  673.1 22.7 %collective-permute-done.40 = bf16[1024,768]{1,0:T(8,128)(2,1)} collective-permute-done((bf16[1024,768]{1,0:T(8,128)(2,1)}, bf16[1024,768]{1,0:T(8,128)(2,1)}, u32[]{:S(2)}, u32[]{:S(2)}) %collective-permute-start.40) | collective-permute-done | bytes 1572896 | tf_op jit(solution)/shard_map/ppermute | solution.py:29
  695.8 31.6 %collective-permute-done.42 = bf16[1024,768]{1,0:T(8,128)(2,1)} collective-permute-done((bf16[1024,768]{1,0:T(8,128)(2,1)}, bf16[1024,768]{1,0:T(8,128)(2,1)}, u32[]{:S(2)}, u32[]{:S(2)}) %collective-permute-start.42) | collective-permute-done | bytes 1572896 | tf_op jit(solution)/shard_map/ppermute | solution.py:29
  727.4 9.3 add_convert_fusion
  736.9 10.9 convolution_convert_fusion
  749.2 46.1 %reduce-scatter.5.cloned.1.call-done = bf16[512,768]{1,0:T(8,128)(2,1)} async-done(((bf16[2048,768]{1,0:T(8,128)(2,1)}), bf16[512,768]{1,0:T(8,128)(2,1)}) %reduce-scatter.5.cloned.1.call-update) | async-done | bytes 786448 | tf_op jit(solution)/shard_map/reduce_scatter | solution.py:306
  798.7 101.9 %reduce-scatter.9.cloned.1.call-done = bf16[512,1408]{1,0:T(8,128)(2,1)} async-done(((bf16[2048,1408]{1,0:T(8,128)(2,1)}), bf16[512,1408]{1,0:T(8,128)(2,1)}) %reduce-scatter.9.cloned.1.call-update) | async-done | bytes 1441808 | tf_op jit(solution)/shard_map/reduce_scatter | solution.py:299
  914.4 7.8 fusion.181
  922.2 7.7 fusion.179
  929.9 7.7 fusion.180
  937.6 11.8 add_add_fusion
  962.2 10.7 collective-permute-done.23
  1000.2 71.6 %all-gather.1 = f32[32,2,2048]{2,1,0:T(2,128)S(1)} all-gather(f32[1,2,2048]{2,1,0:T(2,128)S(1)} %maximum_bitcast_fusion), channel_id=2, replica_groups=mesh['rep'=8,'shard'=4] {'rep','shard'}, dimensions={0}, use_global_device_ids=true | all-gather | bytes 540672 | tf_op jit(solution)/shard_map/all_gather | solution.py:315
  1082.9 8.7 convert_element_type.490
  1104.2 22.5 %all-gather.30.cloned.1.call-done = bf16[512,5632]{0,1:T(8,128)(2,1)} async-done(((bf16[512,704]{0,1:T(8,128)(2,1)}), bf16[512,5632]{0,1:T(8,128)(2,1)}) %all-gather.30.cloned.1.call-update) | async-done | bytes 5767184 | tf_op jit(solution)/shard_map/all_gather | solution.py:297
  1126.7 9.1 copy.333
  1135.8 36.2 %all-gather.32.cloned.1.call-done = bf16[512,5632]{0,1:T(8,128)(2,1)} async-done(((bf16[512,704]{0,1:T(8,128)(2,1)}), bf16[512,5632]{0,1:T(8,128)(2,1)}) %all-gather.32.cloned.1.call-update) | async-done | bytes 5767184 | tf_op jit(solution)/shard_map/all_gather | solution.py:297
  1172.0 9.2 copy.334
  (634 shorter events, 465.4 us)
Async XLA Ops:
  7.2 33.6 %all-gather.16.cloned.1.call-start = ((), (), s32[]{:S(2)}) async-start(), calls=%async_computation.5 | async-start | bytes 1310720 | tf_op jit(solution)/shard_map/all_gather | solution.py:229
  9.5 96.5 %all-gather.14.cloned.1.call-start = ((), (), s32[]{:S(2)}) async-start(), calls=%async_computation.4 | async-start | bytes 3932160 | tf_op jit(solution)/shard_map/all_gather | solution.py:228
  12.7 376.6 %all-gather.18.cloned.1.call-start = ((), (), s32[]{:S(2)}) async-start(), calls=%async_computation.6 | async-start | bytes 7208960 | tf_op jit(solution)/shard_map/all_gather | solution.py:233
  18.9 88.6 %collective-permute-start.4 = (s32[1,512]{1,0:T(1,128)S(1)}, s32[1,512]{1,0:T(1,128)S(1)}, u32[]{:S(2)}, u32[]{:S(2)}) collective-permute-start(s32[1,512]{1,0:T(1,128)S(1)} %copy-done.131), channel_id=1, source_target_pairs={{0,4},{4,0},{8,12},{12,8},{16,20},{20,16},{24,28},{28,24},{1,5},{5... | collective-permute-start | bytes 6152 | tf_op jit(solution)/shard_map/ppermute | solution.py:29
  25.4 164.0 %collective-permute-start.3 = (bf16[512,2048]{1,0:T(8,128)(2,1)}, bf16[512,2048]{1,0:T(8,128)(2,1)}, u32[]{:S(2)}, u32[]{:S(2)}) collective-permute-start(bf16[512,2048]{1,0:T(8,128)(2,1)} %fusion.2), channel_id=1, source_target_pairs={{0,4},{4,0},{8,12},{12,8},{16,20},{20,16},{24,28},{28,24},{1,5},{5... | collective-permute-start | bytes 6291464 | tf_op jit(solution)/shard_map/ppermute | solution.py:29
  40.9 67.1 %collective-permute-start.9 = (bf16[256,2048]{1,0:T(8,128)(2,1)}, bf16[256,2048]{1,0:T(8,128)(2,1)}, u32[]{:S(2)}, u32[]{:S(2)}) collective-permute-start(bf16[256,2048]{1,0:T(8,128)(2,1)} %all-gather.16.cloned.1.call-done), channel_id=1, source_target_pairs={{0,8},{4,12},{8,0},{12,4},{16,24},{20,28},{24,16},{28,20},{1,9},{5... | collective-permute-start | bytes 3145736 | tf_op jit(solution)/shard_map/ppermute | solution.py:29
  45.0 396.7 %all-gather.20.cloned.1.call-start = ((), (), s32[]{:S(2)}) async-start(), calls=%async_computation.7 | async-start | bytes 3604480 | tf_op jit(solution)/shard_map/all_gather | solution.py:234
  45.1 66.8 %collective-permute-start.10 = (bf16[256,2048]{1,0:T(8,128)(2,1)}, bf16[256,2048]{1,0:T(8,128)(2,1)}, u32[]{:S(2)}, u32[]{:S(2)}) collective-permute-start(bf16[256,2048]{1,0:T(8,128)(2,1)} %all-gather.16.cloned.1.call-done), channel_id=1, source_target_pairs={{0,16},{4,20},{8,24},{12,28},{16,0},{20,4},{24,8},{28,12},{1,17},{... | collective-permute-start | bytes 3145736 | tf_op jit(solution)/shard_map/ppermute | solution.py:29
  106.0 104.2 %collective-permute-start.5 = (bf16[2048,768]{1,0:T(8,128)(2,1)}, bf16[2048,768]{1,0:T(8,128)(2,1)}, u32[]{:S(2)}, u32[]{:S(2)}) collective-permute-start(bf16[2048,768]{1,0:T(8,128)(2,1)} %all-gather.14.cloned.1.call-done), channel_id=1, source_target_pairs={{0,8},{4,12},{8,0},{12,4},{16,24},{20,28},{24,16},{28,20},{1,9},{5... | collective-permute-start | bytes 9437192 | tf_op jit(solution)/shard_map/ppermute | solution.py:29
  113.0 74.2 %collective-permute-start.12 = (bf16[128,2048]{1,0:T(8,128)(2,1)S(1)}, bf16[128,2048]{1,0:T(8,128)(2,1)S(1)}, u32[]{:S(2)}, u32[]{:S(2)}) collective-permute-start(bf16[128,2048]{1,0:T(8,128)(2,1)S(1)} %slice.473), channel_id=1, source_target_pairs={{0,8},{4,12},{8,0},{12,4},{16,24},{20,28},{24,16},{28,20},{1,9},{5... | collective-permute-start | bytes 1572872 | tf_op jit(solution)/shard_map/ppermute | solution.py:29
  115.0 106.0 %collective-permute-start.6 = (bf16[2048,768]{1,0:T(8,128)(2,1)}, bf16[2048,768]{1,0:T(8,128)(2,1)}, u32[]{:S(2)}, u32[]{:S(2)}) collective-permute-start(bf16[2048,768]{1,0:T(8,128)(2,1)} %all-gather.14.cloned.1.call-done), channel_id=1, source_target_pairs={{0,16},{4,20},{8,24},{12,28},{16,0},{20,4},{24,8},{28,12},{1,17},{... | collective-permute-start | bytes 9437192 | tf_op jit(solution)/shard_map/ppermute | solution.py:29
  212.9 52.7 %collective-permute-start.7 = (bf16[1024,768]{1,0:T(8,128)(2,1)}, bf16[1024,768]{1,0:T(8,128)(2,1)}, u32[]{:S(2)}, u32[]{:S(2)}) collective-permute-start(bf16[1024,768]{1,0:T(8,128)(2,1)} %slice.463), channel_id=1, source_target_pairs={{0,16},{4,20},{8,24},{12,28},{16,0},{20,4},{24,8},{28,12},{1,17},{... | collective-permute-start | bytes 4718600 | tf_op jit(solution)/shard_map/ppermute | solution.py:29
  233.8 35.3 %collective-permute-start.8 = (bf16[1024,768]{1,0:T(8,128)(2,1)}, bf16[1024,768]{1,0:T(8,128)(2,1)}, u32[]{:S(2)}, u32[]{:S(2)}) collective-permute-start(bf16[1024,768]{1,0:T(8,128)(2,1)} %slice.464), channel_id=1, source_target_pairs={{0,8},{4,12},{8,0},{12,4},{16,24},{20,28},{24,16},{28,20},{1,9},{5... | collective-permute-start | bytes 4718600 | tf_op jit(solution)/shard_map/ppermute | solution.py:29
  383.7 364.2 %reduce-scatter.7.cloned.1.call-start = ((), (), s32[]{:S(2)}) async-start(), calls=%async_computation.12 | async-start | bytes 1310720 | tf_op jit(solution)/shard_map/reduce_scatter | solution.py:304
  539.3 209.3 %reduce-scatter.11.cloned.1.call-start = ((), (), s32[]{:S(2)}) async-start(), calls=%async_computation.17 | async-start | bytes 3604480 | tf_op jit(solution)/shard_map/reduce_scatter | solution.py:300
  547.1 248.2 %reduce-scatter.5.cloned.1.call-start = ((), (), s32[]{:S(2)}) async-start(), calls=%async_computation.8 | async-start | bytes 3932160 | tf_op jit(solution)/shard_map/reduce_scatter | solution.py:306
  623.0 37.6 %collective-permute-start.41 = (bf16[1024,768]{1,0:T(8,128)(2,1)}, bf16[1024,768]{1,0:T(8,128)(2,1)}, u32[]{:S(2)}, u32[]{:S(2)}) collective-permute-start(bf16[1024,768]{1,0:T(8,128)(2,1)} %get-tuple-element.55), channel_id=1, source_target_pairs={{0,16},{4,20},{8,24},{12,28},{16,0},{20,4},{24,8},{28,12},{1,17},{... | collective-permute-start | bytes 4718600 | tf_op jit(solution)/shard_map/ppermute | solution.py:29
  624.5 40.8 %collective-permute-start.43 = (bf16[1024,768]{1,0:T(8,128)(2,1)}, bf16[1024,768]{1,0:T(8,128)(2,1)}, u32[]{:S(2)}, u32[]{:S(2)}) collective-permute-start(bf16[1024,768]{1,0:T(8,128)(2,1)} %get-tuple-element.54), channel_id=1, source_target_pairs={{0,8},{4,12},{8,0},{12,4},{16,24},{20,28},{24,16},{28,20},{1,9},{5... | collective-permute-start | bytes 4718600 | tf_op jit(solution)/shard_map/ppermute | solution.py:29
  640.3 55.5 %collective-permute-start.40 = (bf16[1024,768]{1,0:T(8,128)(2,1)}, bf16[1024,768]{1,0:T(8,128)(2,1)}, u32[]{:S(2)}, u32[]{:S(2)}) collective-permute-start(bf16[1024,768]{1,0:T(8,128)(2,1)} %slice.523), channel_id=1, source_target_pairs={{0,8},{4,12},{8,0},{12,4},{16,24},{20,28},{24,16},{28,20},{1,9},{5... | collective-permute-start | bytes 4718600 | tf_op jit(solution)/shard_map/ppermute | solution.py:29
  650.0 45.8 %collective-permute-start.45 = (bf16[1024,768]{1,0:T(8,128)(2,1)}, bf16[1024,768]{1,0:T(8,128)(2,1)}, u32[]{:S(2)}, u32[]{:S(2)}) collective-permute-start(bf16[1024,768]{1,0:T(8,128)(2,1)} %slice.528), channel_id=1, source_target_pairs={{0,16},{4,20},{8,24},{12,28},{16,0},{20,4},{24,8},{28,12},{1,17},{... | collective-permute-start | bytes 4718600 | tf_op jit(solution)/shard_map/ppermute | solution.py:29
  663.7 63.7 %collective-permute-start.42 = (bf16[1024,768]{1,0:T(8,128)(2,1)}, bf16[1024,768]{1,0:T(8,128)(2,1)}, u32[]{:S(2)}, u32[]{:S(2)}) collective-permute-start(bf16[1024,768]{1,0:T(8,128)(2,1)} %add_convert_fusion.5), channel_id=1, source_target_pairs={{0,8},{4,12},{8,0},{12,4},{16,24},{20,28},{24,16},{28,20},{1,9},{5... | collective-permute-start | bytes 4718600 | tf_op jit(solution)/shard_map/ppermute | solution.py:29
  668.4 59.1 %collective-permute-start.44 = (bf16[1024,768]{1,0:T(8,128)(2,1)}, bf16[1024,768]{1,0:T(8,128)(2,1)}, u32[]{:S(2)}, u32[]{:S(2)}) collective-permute-start(bf16[1024,768]{1,0:T(8,128)(2,1)} %add_convert_fusion.4), channel_id=1, source_target_pairs={{0,16},{4,20},{8,24},{12,28},{16,0},{20,4},{24,8},{28,12},{1,17},{... | collective-permute-start | bytes 4718600 | tf_op jit(solution)/shard_map/ppermute | solution.py:29
  736.8 163.8 %reduce-scatter.9.cloned.1.call-start = ((), (), s32[]{:S(2)}) async-start(), calls=%async_computation.14 | async-start | bytes 7208960 | tf_op jit(solution)/shard_map/reduce_scatter | solution.py:299
  747.8 330.9 %all-gather.28.cloned.1.call-start = ((), (), s32[]{:S(2)}) async-start(), calls=%async_computation.13 | async-start | bytes 2359296 | tf_op jit(solution)/shard_map/all_gather | solution.py:297
  748.6 334.4 %all-gather.34.cloned.1.call-start = ((), (), s32[]{:S(2)}) async-start(), calls=%async_computation.18 | async-start | bytes 6488064 | tf_op jit(solution)/shard_map/all_gather | solution.py:297
  749.1 342.5 %all-gather.22.cloned.1.call-start = ((), (), s32[]{:S(2)}) async-start(), calls=%async_computation.9 | async-start | bytes 2359296 | tf_op jit(solution)/shard_map/all_gather | solution.py:297
  797.3 298.6 %all-gather.24.cloned.1.call-start = ((), (), s32[]{:S(2)}) async-start(), calls=%async_computation.10 | async-start | bytes 2359296 | tf_op jit(solution)/shard_map/all_gather | solution.py:297
  797.9 302.2 %all-gather.26.cloned.1.call-start = ((), (), s32[]{:S(2)}) async-start(), calls=%async_computation.11 | async-start | bytes 2359296 | tf_op jit(solution)/shard_map/all_gather | solution.py:297
  798.7 328.1 %all-gather.30.cloned.1.call-start = ((), (), s32[]{:S(2)}) async-start(), calls=%async_computation.15 | async-start | bytes 6488064 | tf_op jit(solution)/shard_map/all_gather | solution.py:297
  903.6 268.4 %all-gather.32.cloned.1.call-start = ((), (), s32[]{:S(2)}) async-start(), calls=%async_computation.16 | async-start | bytes 6488064 | tf_op jit(solution)/shard_map/all_gather | solution.py:297
  914.1 37.1 %collective-permute-start.19 = (bf16[512,2048]{1,0:T(8,128)(2,1)}, bf16[512,2048]{1,0:T(8,128)(2,1)}, u32[]{:S(2)}, u32[]{:S(2)}) collective-permute-start(bf16[512,2048]{1,0:T(8,128)(2,1)} %slice.482), channel_id=1, source_target_pairs={{0,4},{4,0},{8,12},{12,8},{16,20},{20,16},{24,28},{28,24},{1,5},{5... | collective-permute-start | bytes 6291464 | tf_op jit(solution)/shard_map/ppermute | solution.py:29
  951.0 44.8 %collective-permute-start.39 = (bf16[512,2048]{1,0:T(8,128)(2,1)}, bf16[512,2048]{1,0:T(8,128)(2,1)}, u32[]{:S(2)}, u32[]{:S(2)}) collective-permute-start(bf16[512,2048]{1,0:T(8,128)(2,1)} %slice.618), channel_id=1, source_target_pairs={{0,4},{4,0},{8,12},{12,8},{16,20},{20,16},{24,28},{28,24},{1,5},{5... | collective-permute-start | bytes 6291464 | tf_op jit(solution)/shard_map/ppermute | solution.py:29
  (174 other events, 2087.2 us)
Sparse Core Ops, SparseCore 0:
  10.2 30.6 all-gather.15
  43.0 62.9 all-gather.13
  107.6 105.3 all-gather.17
  383.8 57.9 all-gather.19
  539.5 25.8 reduce-scatter.6
  567.6 54.8 reduce-scatter.10
  736.9 58.3 reduce-scatter.4
  798.3 102.2 reduce-scatter.8
  902.6 28.3 all-gather.27
  933.0 56.7 all-gather.33
  991.8 28.9 all-gather.21
  1022.7 28.5 all-gather.23
  1053.3 28.1 all-gather.25
  1083.4 43.3 all-gather.29
  1128.6 43.3 all-gather.31
